TPU v7x, 32 devices: a whole 2x2x4 slice. The times are simulated.
32 devices in a mesh: groups: 2 (over x), ctx: 16 (over z, y, core).
Axes of the slice: x: 2, y: 2, z: 4, core: 2. Of those that a mesh axis runs over, the one named last changes fastest.
Arguments:
- raster_tokens: bfloat16 [4096, 1024], P(('groups', 'ctx')), parts along dimension 0, may hold values from -45 to 45
- hilbert_perm: int32 [4096], P(('groups', 'ctx')), parts along dimension 0, may hold values from 0 to 2047, as said below
- neighbors: int32 [32, 5], P(('groups', 'ctx')), parts along dimension 0, may hold values from 0 to 15, as said below
- neighbor_counts: int32 [32], P(('groups', 'ctx')), parts along dimension 0, may hold values from 1 to 5, as said below
- norm_gain: float32 [1024], replicated, may hold values from 0.1 to 1.9
- w_qkv: bfloat16 [1024, 3072], replicated, may hold values from -0.8125 to 0.8125
- w_out: bfloat16 [1024, 1024], replicated, may hold values from -0.5 to 0.5
- cotangent: bfloat16 [4096, 1024], P(('groups', 'ctx')), parts along dimension 0, may hold values from -6 to 6
Outputs:
- layer_out: bfloat16 [4096, 1024], P(('groups', 'ctx')), parts along dimension 0
- grad_tokens: bfloat16 [4096, 1024], P(('groups', 'ctx')), parts along dimension 0
- grad_w_out: float32 [2048, 1024], P(('groups', 'ctx')), parts along dimension 0
- grad_gain: float32 [2048], P('groups'), parts along dimension 0
There are 2 independent parts, one for each index of `groups`. A program takes and returns all parts, laid end to end along the dimension named above; an argument that names none is the same for every part. Nothing has to cross between parts.
Inputs may be any that keep to these rules, and one draw needn't show every extreme that they name: `hilbert_perm`: A permutation. Every 128 consecutive positions of the Hilbert order take exactly 8 tokens from every 128 consecutive raster tokens. `neighbors`: row b starts with b, followed by distinct blocks other than b at a distance of at most 4; entries from slot neighbor_counts[b] on equal b. `neighbor_counts`: the block itself is counted.
All inputs are finite; a program needn't handle non-finite values.
Results may differ from a plain program's by a relative error of at most 0.02.
The roundings to bfloat16 on the way count: a program that leaves them out, or rounds other values in their place, can miss the bound.
Values may be sent and summed in bfloat16 or wider, within the bound.
No kernel may reach another device: no remote copies, remote signals or barrier semaphores. Data moves between devices by JAX's collectives and lax.ppermute only.
A program may use at most 128 MiB of HBM per device.

v0:
```python
import jax
import jax.numpy as jnp
from jax import lax
from jax.sharding import PartitionSpec as P

HEADS = 16
BLOCK = 128
REACH = 4
EPS = 1e-06
FAR = -1e30


def from_behind(block, axis, distance):
    devices = range(lax.axis_size(axis))
    route = [(i - distance, i) for i in devices if i - distance in devices]
    return lax.ppermute(block, axis, route)


def softmax_probs(heads_q, heads_k, counts, score_scale):
    scores = (
        jnp.einsum("sqhd,skhd->shqk", heads_q, heads_k, preferred_element_type=jnp.float32)
        * score_scale
    )
    slot_of = jnp.arange(heads_k.shape[1]) // BLOCK
    usable = slot_of[None, :] < counts[:, None]
    scores = jnp.where(usable[:, None, None, :], scores, FAR)
    row_max = jnp.max(scores, axis=-1, keepdims=True)
    shifted = jnp.exp(scores - row_max)
    return shifted / jnp.sum(shifted, axis=-1, keepdims=True)


def per_device(
    raster_tokens, hilbert_perm, neighbors, neighbor_counts, norm_gain, w_qkv, w_out, cotangent
):
    axis_size = lax.axis_size("ctx")
    my_index = lax.axis_index("ctx")
    tok_rows, model_width = raster_tokens.shape
    per_peer = tok_rows // axis_size
    per_dev = tok_rows // BLOCK
    reach_dev = (REACH + per_dev - 1) // per_dev
    head_dim = model_width // HEADS
    score_scale = head_dim ** (-0.5)
    norm_scale = (tok_rows * axis_size) ** (-0.5)
    source_dev = hilbert_perm // tok_rows
    local_row = hilbert_perm % tok_rows
    sorted_rows = jnp.argsort(source_dev, stable=True)
    wanted = local_row[sorted_rows].reshape(axis_size, per_peer)
    requested = lax.all_to_all(wanted, "ctx", split_axis=0, concat_axis=0, tiled=True)
    requested_flat = requested.reshape(-1)
    outgoing = raster_tokens[requested_flat].reshape(axis_size, per_peer, model_width)
    arrived = lax.all_to_all(outgoing, "ctx", split_axis=0, concat_axis=0, tiled=True)
    ordered = (
        jnp.zeros_like(raster_tokens).at[sorted_rows].set(arrived.reshape(tok_rows, model_width))
    )
    ordered_f = ordered.astype(jnp.float32)
    inv_rms = lax.rsqrt(jnp.mean(ordered_f * ordered_f, axis=-1, keepdims=True) + EPS)
    normed = (ordered_f * inv_rms * norm_gain).astype(jnp.bfloat16)
    projected = jnp.dot(normed, w_qkv, preferred_element_type=jnp.float32).astype(jnp.bfloat16)
    queries = projected[:, :model_width]
    keys_vals = projected[:, model_width:]
    kv_weight = w_qkv[:, model_width:]
    from_lower = []
    from_upper = []
    carry_low = normed
    carry_high = normed
    for distance in range(reach_dev):
        carry_low = from_behind(carry_low, "ctx", 1)
        carry_high = from_behind(carry_high, "ctx", -1)
        from_lower.append(carry_low)
        from_upper.append(carry_high)
    remote_low = [
        jnp.dot(remote_piece, kv_weight, preferred_element_type=jnp.float32).astype(jnp.bfloat16)
        for remote_piece in from_lower
    ]
    remote_high = [
        jnp.dot(remote_piece, kv_weight, preferred_element_type=jnp.float32).astype(jnp.bfloat16)
        for remote_piece in from_upper
    ]
    window = jnp.concatenate(remote_low[::-1] + [keys_vals] + remote_high, axis=0)
    window_blocks = window.reshape(-1, BLOCK, 2 * model_width)
    slot_index = neighbors - (my_index - reach_dev) * per_dev
    gathered = window_blocks[slot_index].reshape(per_dev, -1, 2 * model_width)
    heads_k = gathered[:, :, :model_width].reshape(per_dev, -1, HEADS, head_dim)
    heads_v = gathered[:, :, model_width:].reshape(per_dev, -1, HEADS, head_dim)
    heads_q = queries.reshape(per_dev, BLOCK, HEADS, head_dim)
    weights_f = softmax_probs(heads_q, heads_k, neighbor_counts, score_scale)
    probs_b = weights_f.astype(jnp.bfloat16)
    attended = jnp.einsum("shqk,skhd->sqhd", probs_b, heads_v, preferred_element_type=jnp.float32)
    attended = attended.reshape(tok_rows, model_width).astype(jnp.bfloat16)
    projected_out = jnp.dot(attended, w_out, preferred_element_type=jnp.float32)
    layer_out = (ordered_f + projected_out).astype(jnp.bfloat16)
    grad_w_out = None
    d_attended = jnp.dot(cotangent, w_out.T, preferred_element_type=jnp.float32).astype(
        jnp.bfloat16
    )
    d_heads = d_attended.reshape(per_dev, BLOCK, HEADS, head_dim)
    d_probs = jnp.einsum("sqhd,skhd->shqk", d_heads, heads_v, preferred_element_type=jnp.float32)
    row_dots = jnp.sum(d_probs * weights_f, axis=-1, keepdims=True)
    d_scores = (weights_f * (d_probs - row_dots) * score_scale).astype(jnp.bfloat16)
    d_query = jnp.einsum("shqk,skhd->sqhd", d_scores, heads_k, preferred_element_type=jnp.float32)
    d_query = d_query.reshape(tok_rows, model_width).astype(jnp.bfloat16)
    d_keys = jnp.einsum("shqk,sqhd->skhd", d_scores, heads_q, preferred_element_type=jnp.float32)
    d_vals = jnp.einsum("shqk,sqhd->skhd", probs_b, d_heads, preferred_element_type=jnp.float32)
    contrib = jnp.concatenate(
        [d_keys.reshape(-1, BLOCK, model_width), d_vals.reshape(-1, BLOCK, model_width)], axis=-1
    )
    summed = jnp.zeros(window_blocks.shape, jnp.float32).at[slot_index.reshape(-1)].add(contrib)
    partials = summed.astype(jnp.bfloat16)
    accum = partials[reach_dev].astype(jnp.float32)
    for distance in range(1, reach_dev + 1):
        accum = accum + from_behind(partials[reach_dev + distance], "ctx", distance).astype(
            jnp.float32
        )
        accum = accum + from_behind(partials[reach_dev - distance], "ctx", -distance).astype(
            jnp.float32
        )
    d_kv = accum.astype(jnp.bfloat16)
    d_proj = jnp.concatenate([d_query, d_kv], axis=-1)
    d_normed = jnp.dot(d_proj, w_qkv.T, preferred_element_type=jnp.float32)
    gain_term = jnp.sum(d_normed * ordered_f * inv_rms, axis=0)
    grad_gain = lax.psum(gain_term, "ctx") * norm_scale
    scaled = d_normed * norm_gain
    d_ordered = (
        cotangent.astype(jnp.float32)
        + inv_rms * scaled
        - ordered_f * inv_rms**3 * jnp.mean(scaled * ordered_f, axis=-1, keepdims=True)
    )
    d_ordered = d_ordered.astype(jnp.bfloat16)
    leaving = d_ordered[sorted_rows].reshape(axis_size, per_peer, model_width)
    returned = lax.all_to_all(leaving, "ctx", split_axis=0, concat_axis=0, tiled=True)
    grad_tokens = (
        jnp.zeros_like(raster_tokens)
        .at[requested_flat]
        .set(returned.reshape(tok_rows, model_width))
    )
    grad_w_out = (
        lax.psum_scatter(
            lax.dot_general(
                attended, cotangent, (((0,), (0,)), ((), ())), preferred_element_type=jnp.float32
            ),
            "ctx",
            scatter_dimension=0,
            tiled=True,
        )
        * norm_scale
    )
    return (layer_out, grad_tokens, grad_w_out, grad_gain)


def solution(mesh):
    placed = (
        P(("groups", "ctx"), None),
        P(("groups", "ctx")),
        P(("groups", "ctx"), None),
        P(("groups", "ctx")),
        P(),
        P(),
        P(),
        P(("groups", "ctx"), None),
    )
    return jax.shard_map(
        per_device,
        mesh=mesh,
        in_specs=placed,
        out_specs=(
            P(("groups", "ctx"), None),
            P(("groups", "ctx"), None),
            P(("groups", "ctx"), None),
            P("groups"),
        ),
        check_vma=False,
    )
```

profile of v0, /device:TPU:0, one launch (start us, length us, event | category | flops | bytes accessed | tf_op | source)
XLA Modules:
  0.0 316.0 jit_solution(17017370256104363028)
XLA Ops:
  7.2 0.8 and_select_fusion
  8.0 2.5 sort.17
  10.6 1.2 gather_fusion
  11.9 13.6 %all_to_all.19 = s32[16,1,8]{2,1,0:T(1,128)S(1)} all-to-all(s32[16,1,8]{2,1,0:T(1,128)S(1)} %bitcast.117), channel_id=1, replica_groups=mesh['groups'=2,'ctx'=16] {'ctx'}, dimensions={0} | all-to-all | bytes 1024 | tf_op jit(solution)/shard_map/all_to_all | solution.py:48
  26.9 2.0 gather_fusion.1
  28.9 12.6 %all_to_all.20 = bf16[16,8,1024]{2,1,0:T(8,128)(2,1)S(1)} all-to-all(bf16[16,8,1024]{2,1,0:T(8,128)(2,1)S(1)} %bitcast.109), channel_id=1, replica_groups=mesh['groups'=2,'ctx'=16] {'ctx'}, dimensions={0} | all-to-all | bytes 524288 | tf_op jit(solution)/shard_map/all_to_all | solution.py:51
  41.5 1.2 scatter_custom_fusion
  42.9 0.8 fusion.60
  43.7 1.8 collective-permute-start
  45.5 1.3 collective-permute-start.4
  46.8 4.6 %collective-permute-start.1 = (bf16[128,1024]{1,0:T(8,128)(2,1)S(1)}, bf16[128,1024]{1,0:T(8,128)(2,1)}, u32[]{:S(2)}, u32[]{:S(2)}) collective-permute-start(bf16[128,1024]{1,0:T(8,128)(2,1)S(1)} %collective-permute-done), channel_id=1, source_target_pairs={{0,1},{1,2},{2,3},{3,4},{4,5},{5,6},{6,7},{7,8},{8,9},{9,10},{10,1... | collective-permute-start | bytes 786440 | tf_op jit(solution)/shard_map/ppermute | solution.py:16
  51.4 1.3 collective-permute-start.5
  52.7 6.4 %collective-permute-start.2 = (bf16[128,1024]{1,0:T(8,128)(2,1)}, bf16[128,1024]{1,0:T(8,128)(2,1)}, u32[]{:S(2)}, u32[]{:S(2)}) collective-permute-start(bf16[128,1024]{1,0:T(8,128)(2,1)} %collective-permute-done.1), channel_id=1, source_target_pairs={{0,1},{1,2},{2,3},{3,4},{4,5},{5,6},{6,7},{7,8},{8,9},{9,10},{10,1... | collective-permute-start | bytes 786440 | tf_op jit(solution)/shard_map/ppermute | solution.py:16
  59.8 1.3 collective-permute-start.6
  61.1 6.1 %collective-permute-start.3 = (bf16[128,1024]{1,0:T(8,128)(2,1)}, bf16[128,1024]{1,0:T(8,128)(2,1)}, u32[]{:S(2)}, u32[]{:S(2)}) collective-permute-start(bf16[128,1024]{1,0:T(8,128)(2,1)} %collective-permute-done.2), channel_id=1, source_target_pairs={{0,1},{1,2},{2,3},{3,4},{4,5},{5,6},{6,7},{7,8},{8,9},{9,10},{10,1... | collective-permute-start | bytes 786440 | tf_op jit(solution)/shard_map/ppermute | solution.py:16
  67.2 3.8 %convolution_convert_fusion = bf16[128,3072]{1,0:T(8,128)(2,1)S(1)} fusion(bf16[128,1024]{1,0:T(8,128)(2,1)S(1)} %fusion.60, bf16[1024,3072]{1,0:T(8,128)(2,1)} %param.13), kind=kOutput, calls=%fused_computation.16 | convolution fusion | flops 805699584 | bytes 7340032 | tf_op jit(solution)/shard_map/dot_general | solution.py:58
  71.0 0.8 copy.27
  71.9 1.3 collective-permute-start.7
  73.2 3.1 fusion.24
  76.3 3.1 fusion.23
  79.5 3.0 fusion.22
  82.6 0.7 fusion.21
  84.2 1.7 fusion.19
  85.9 1.7 fusion.18
  88.4 2.1 copy-done.3
  90.5 4.7 %gather_fusion.2 = bf16[5,128,2048]{2,1,0:T(8,128)(2,1)} fusion(bf16[9,128,2048]{2,1,0:T(8,128)(2,1)} %bitcast.106, s32[1024]{0:T(1024)S(1)} %pad_clamp_fusion), kind=kCustom, calls=%fused_computation.2 | custom fusion | bytes 5242900 | tf_op jit(solution)/shard_map/gather | solution.py:82
  95.2 3.5 %fusion.89 = (bf16[1,640,1024]{2,1,0:T(8,128)(2,1)}, bf16[1,640,1024]{2,1,0:T(8,128)(2,1)}) fusion(bf16[1,640,2048]{2,1,0:T(8,128)(2,1)} %bitcast.103), kind=kLoop, calls=%fused_computation.138 | loop fusion | bytes 5242880 | tf_op jit(solution)/shard_map/slice | solution.py:83
  98.7 2.5 copy.33
  101.1 2.5 copy.32
  103.6 5.5 %fusion.90 = (f32[16,128]{1,0:T(8,128)S(1)}, f32[16,128,640]{2,1,0:T(8,128)}) fusion(pred[640]{0:T(1024)(128)(4,1)S(1)} %fusion.75, bf16[128,16,64]{0,2,1:T(8,128)(2,1)S(1)} %bitcast.114, bf16[640,16,64]{0,2,1:T(8,128)(2,1)} %bitcast.107), kind=kOutput, calls=%fused_computation.139 | convolution fusion | flops 173015680 | bytes 6824576 | tf_op jit(solution)/shard_map/sub | solution.py:28
  109.2 4.1 %fusion.31 = bf16[16,64,128]{2,1,0:T(8,128)(2,1)S(1)} fusion(bf16[640,16,64]{0,2,1:T(8,128)(2,1)} %bitcast.104, f32[16,128,640]{2,1,0:T(8,128)} %get-tuple-element.23, f32[16,128]{1,0:T(8,128)S(1)} %get-tuple-element.22), kind=kOutput, calls=%fused_computation.47 | convolution fusion | flops 170524672 | bytes 6823936 | tf_op jit(solution)/shard_map/shqk,skhd->sqhd/dot_general | solution.py:88
  113.3 2.7 fusion.92
  116.0 0.8 convolution_convert_fusion.9
  117.0 4.6 %convolution_bitcast_fusion = f32[1,640,16,64]{1,3,2,0:T(8,128)} fusion(bf16[128,16,64]{0,2,1:T(8,128)(2,1)S(1)} %bitcast.112, f32[16,128,640]{2,1,0:T(8,128)} %get-tuple-element.23, f32[16,128]{1,0:T(8,128)S(1)} %get-tuple-element.22), kind=kOutput, calls=%fused_computation.42 | convolution fusion | flops 170393600 | bytes 8134656 | tf_op jit(solution)/shard_map/shqk,sqhd->skhd/dot_general | solution.py:103
  121.6 4.4 %reshape.226 = f32[5,128,1024]{1,0,2:T(8,128)} reshape(f32[1,640,16,64]{1,3,2,0:T(8,128)} %convolution_bitcast_fusion) | data formatting | bytes 5242880 | tf_op jit(solution)/shard_map/reshape | solution.py:105
  126.0 4.6 %fusion.91 = f32[16,128,640]{2,1,0:T(8,128)} fusion(bf16[128,16,64]{0,2,1:T(8,128)(2,1)S(1)} %bitcast.113, bf16[640,16,64]{0,2,1:T(8,128)(2,1)} %bitcast.105), kind=kOutput, calls=%fused_computation.140 | convolution fusion | flops 167772160 | bytes 6815744 | tf_op jit(solution)/shard_map/sqhd,skhd->shqk/dot_general | solution.py:97
  130.6 19.2 %fusion.25 = f32[1,640,16,64]{1,3,2,0:T(8,128)} fusion(bf16[128,16,64]{0,2,1:T(8,128)(2,1)S(1)} %bitcast.115, f32[16,128,640]{2,1,0:T(8,128)} %fusion.91, f32[16,128,640]{2,1,0:T(8,128)} %get-tuple-element.23, f32[16,128]{1,0:T(8,128)S(1)} %get-tuple-element.22), kind=kOutput, calls=%fused_computation.41 | convolution fusion | flops 176949888 | bytes 13377536 | tf_op jit(solution)/shard_map/shqk,sqhd->skhd/dot_general | solution.py:102
  149.9 4.4 %reshape.225 = f32[5,128,1024]{1,0,2:T(8,128)} reshape(f32[1,640,16,64]{1,3,2,0:T(8,128)} %fusion.25) | data formatting | bytes 5242880 | tf_op jit(solution)/shard_map/reshape | solution.py:105
  154.3 6.7 %pad_maximum_fusion = f32[5,128,2048]{1,0,2:T(8,128)} fusion(f32[5,128,1024]{1,0,2:T(8,128)} %reshape.226, f32[5,128,1024]{1,0,2:T(8,128)} %reshape.225), kind=kLoop, calls=%fused_computation.9 | loop fusion | flops 1310720 | bytes 10485760 | tf_op jit(solution)/shard_map/concatenate | solution.py:104
  161.0 7.9 %copy.30 = f32[5,128,2048]{2,1,0:T(8,128)} copy(f32[5,128,2048]{1,0,2:T(8,128)} %pad_maximum_fusion) | data formatting | bytes 10485760 | tf_op jit(solution)/shard_map/concatenate | solution.py:104
  168.9 4.8 %broadcast_in_dim.22 = f32[9,128,2048]{2,1,0:T(8,128)} broadcast(f32[]{:T(128)} %constant.63.clone.1), dimensions={} | broadcast | bytes 9437188 | tf_op jit(solution)/shard_map/broadcast_in_dim | solution.py:107
  173.7 11.9 %scatter_fusion = f32[9,128,2048]{2,1,0:T(8,128)} fusion(f32[9,128,2048]{2,1,0:T(8,128)} %broadcast_in_dim.22, s32[5]{0:T(128)S(1)} %fusion.81, f32[5,128,2048]{2,1,0:T(8,128)} %copy.30), kind=kCustom, calls=%fused_computation.5 | custom fusion | flops 1310720 | bytes 15728660 | tf_op jit(solution)/shard_map/scatter-add | solution.py:107
  185.7 4.4 %convert_element_type.137 = bf16[9,128,2048]{2,1,0:T(8,128)(2,1)S(1)} convert(f32[9,128,2048]{2,1,0:T(8,128)} %scatter_fusion) | non-fusion elementwise | flops 2359296 | bytes 14155776 | tf_op jit(solution)/shard_map/convert_element_type | solution.py:108
  190.1 2.1 copy-done.1
  192.2 1.6 slice_bitcast_fusion.7
  193.8 5.4 %collective-permute-start.8 = (bf16[128,2048]{1,0:T(8,128)(2,1)S(1)}, bf16[128,2048]{1,0:T(8,128)(2,1)}, u32[]{:S(2)}, u32[]{:S(2)}) collective-permute-start(bf16[128,2048]{1,0:T(8,128)(2,1)S(1)} %get-tuple-element.8), channel_id=1, source_target_pairs={{0,1},{1,2},{2,3},{3,4},{4,5},{5,6},{6,7},{7,8},{8,9},{9,10},{10,1... | collective-permute-start | bytes 1572872 | tf_op jit(solution)/shard_map/ppermute | solution.py:16
  199.3 1.3 collective-permute-start.15
  200.5 7.8 %collective-permute-start.14 = (bf16[128,2048]{1,0:T(8,128)(2,1)S(1)}, bf16[128,2048]{1,0:T(8,128)(2,1)}, u32[]{:S(2)}, u32[]{:S(2)}) collective-permute-start(bf16[128,2048]{1,0:T(8,128)(2,1)S(1)} %get-tuple-element.10), channel_id=1, source_target_pairs={{0,4},{1,5},{2,6},{3,7},{4,8},{5,9},{6,10},{7,11},{8,12},{9,13},{1... | collective-permute-start | bytes 1572872 | tf_op jit(solution)/shard_map/ppermute | solution.py:16
  208.3 1.5 collective-permute-start.13
  209.8 6.8 %collective-permute-start.12 = (bf16[128,2048]{1,0:T(8,128)(2,1)}, bf16[128,2048]{1,0:T(8,128)(2,1)}, u32[]{:S(2)}, u32[]{:S(2)}) collective-permute-start(bf16[128,2048]{1,0:T(8,128)(2,1)} %get-tuple-element.12), channel_id=1, source_target_pairs={{0,3},{1,4},{2,5},{3,6},{4,7},{5,8},{6,9},{7,10},{8,11},{9,12},{10... | collective-permute-start | bytes 1572872 | tf_op jit(solution)/shard_map/ppermute | solution.py:16
  216.6 1.3 collective-permute-start.11
  218.4 4.9 %collective-permute-start.10 = (bf16[128,2048]{1,0:T(8,128)(2,1)}, bf16[128,2048]{1,0:T(8,128)(2,1)}, u32[]{:S(2)}, u32[]{:S(2)}) collective-permute-start(bf16[128,2048]{1,0:T(8,128)(2,1)} %get-tuple-element.14), channel_id=1, source_target_pairs={{0,2},{1,3},{2,4},{3,5},{4,6},{5,7},{6,8},{7,9},{8,10},{9,11},{10,... | collective-permute-start | bytes 1572872 | tf_op jit(solution)/shard_map/ppermute | solution.py:16
  223.3 1.3 collective-permute-start.9
  224.6 19.1 %fusion.34 = bf16[16,64,128]{2,1,0:T(8,128)(2,1)S(1)} fusion(bf16[640,16,64]{0,2,1:T(8,128)(2,1)} %bitcast.108, f32[16,128,640]{2,1,0:T(8,128)} %fusion.91, f32[16,128,640]{2,1,0:T(8,128)} %get-tuple-element.23, f32[16,128]{1,0:T(8,128)S(1)} %get-tuple-element.22), kind=kOutput, calls=%fused_computation.48 | convolution fusion | flops 177080960 | bytes 12066816 | tf_op jit(solution)/shard_map/shqk,skhd->sqhd/dot_general | solution.py:100
  243.9 1.9 collective-permute-done.12
  245.8 9.2 %collective-permute-done.10 = bf16[128,2048]{1,0:T(8,128)(2,1)} collective-permute-done((bf16[128,2048]{1,0:T(8,128)(2,1)}, bf16[128,2048]{1,0:T(8,128)(2,1)}, u32[]{:S(2)}, u32[]{:S(2)}) %collective-permute-start.10) | collective-permute-done | bytes 524320 | tf_op jit(solution)/shard_map/ppermute | solution.py:16
  255.0 3.1 fusion.45
  258.0 5.1 %fusion.66 = (f32[1024]{0:T(1024)S(1)}, f32[128]{0:T(128)S(1)}, f32[128,1024]{1,0:T(8,128)S(1)}) fusion(bf16[128,1024]{1,0:T(8,128)(2,1)S(1)} %scatter_custom_fusion, f32[128]{0:T(128)S(1)} %get-tuple-element.19, f32[1024]{0:T(1024)S(1)} %copy-done.6, bf16[1024,3072]{1,0:T(8,128)(2,1)} %param.13, bf16[128,2048]{1,0:T(8,128)(2,1)S(1)} %fusion.45, ...), kind=kOutput, calls=%fused_computation.85 | convolution fusion | flops 807795584 | bytes 7873536 | tf_op jit(solution)/shard_map/dot_general | solution.py:119
  263.4 1.6 gather_fusion.3
  265.0 5.1 %all-to-all-start.2 = ((bf16[16,8,1024]{2,1,0:T(8,128)(2,1)}), bf16[16,8,1024]{2,1,0:T(8,128)(2,1)S(1)}, u32[]{:S(2)}, u32[]{:S(2)}) async-start(bf16[16,8,1024]{2,1,0:T(8,128)(2,1)} %bitcast.33), calls=%async_computation.2 | async-start | bytes 524288 | tf_op jit(solution)/shard_map/all_to_all | solution.py:130
  270.1 1.2 fusion.37
  271.3 33.8 %psum.7 = f32[1024]{0:T(1024)S(1)} all-reduce(f32[1024]{0:T(1024)S(1)} %get-tuple-element.6), channel_id=1, replica_groups=mesh['groups'=2,'ctx'=16] {'ctx'}, use_global_device_ids=true, to_apply=%region_11.12 | all-reduce | flops 1024 | bytes 8192 | tf_op jit(solution)/shard_map/psum | solution.py:121
  305.7 1.8 scatter_custom_fusion.2
  307.5 1.7 broadcast_multiply_fusion
  (69 shorter events, 5.0 us)
Async XLA Ops:
  7.2 108.8 %copy-start = (bf16[1024,1024]{1,0:T(8,128)(2,1)S(1)}, bf16[1024,1024]{1,0:T(8,128)(2,1)}, u32[]{:S(2)}) copy-start(bf16[1024,1024]{1,0:T(8,128)(2,1)} %param.14) | copy-start | bytes 6291460
  7.2 51.9 %copy-start.11 = (s32[1,5]{1,0:T(1,128)S(1)}, s32[1,5]{1,0:T(1,128)}, u32[]{:S(2)}) copy-start(s32[1,5]{1,0:T(1,128)} %param.10) | copy-start | bytes 64
  7.2 300.3 %reduce-scatter.2.cloned.1.call-start = ((), (), s32[]{:S(2)}) async-start(), calls=%async_computation.4 | async-start | bytes 4456448 | tf_op jit(solution)/shard_map/reduce_scatter | solution.py:137
  43.7 3.1 collective-permute-start
  45.5 5.9 %collective-permute-start.4 = (bf16[128,1024]{1,0:T(8,128)(2,1)S(1)}, bf16[128,1024]{1,0:T(8,128)(2,1)S(1)}, u32[]{:S(2)}, u32[]{:S(2)}) collective-permute-start(bf16[128,1024]{1,0:T(8,128)(2,1)S(1)} %fusion.60), channel_id=1, source_target_pairs={{1,0},{2,1},{3,2},{4,3},{5,4},{6,5},{7,6},{8,7},{9,8},{10,9},{11,1... | collective-permute-start | bytes 786440 | tf_op jit(solution)/shard_map/ppermute | solution.py:16
  46.8 14.3 %copy-start.9 = (bf16[128,1024]{1,0:T(8,128)(2,1)}, bf16[128,1024]{1,0:T(8,128)(2,1)S(1)}, u32[]{:S(2)}) copy-start(bf16[128,1024]{1,0:T(8,128)(2,1)S(1)} %collective-permute-done) | copy-start | bytes 786436
  46.8 5.9 %collective-permute-start.1 = (bf16[128,1024]{1,0:T(8,128)(2,1)S(1)}, bf16[128,1024]{1,0:T(8,128)(2,1)}, u32[]{:S(2)}, u32[]{:S(2)}) collective-permute-start(bf16[128,1024]{1,0:T(8,128)(2,1)S(1)} %collective-permute-done), channel_id=1, source_target_pairs={{0,1},{1,2},{2,3},{3,4},{4,5},{5,6},{6,7},{7,8},{8,9},{9,10},{10,1... | collective-permute-start | bytes 786440 | tf_op jit(solution)/shard_map/ppermute | solution.py:16
  51.4 9.7 %copy-start.7 = (bf16[128,1024]{1,0:T(8,128)(2,1)}, bf16[128,1024]{1,0:T(8,128)(2,1)S(1)}, u32[]{:S(2)}) copy-start(bf16[128,1024]{1,0:T(8,128)(2,1)S(1)} %collective-permute-done.4) | copy-start | bytes 786436
  51.4 8.4 %collective-permute-start.5 = (bf16[128,1024]{1,0:T(8,128)(2,1)S(1)}, bf16[128,1024]{1,0:T(8,128)(2,1)}, u32[]{:S(2)}, u32[]{:S(2)}) collective-permute-start(bf16[128,1024]{1,0:T(8,128)(2,1)S(1)} %collective-permute-done.4), channel_id=1, source_target_pairs={{1,0},{2,1},{3,2},{4,3},{5,4},{6,5},{7,6},{8,7},{9,8},{10,9},{11,1... | collective-permute-start | bytes 786440 | tf_op jit(solution)/shard_map/ppermute | solution.py:16
  52.7 8.4 %collective-permute-start.2 = (bf16[128,1024]{1,0:T(8,128)(2,1)}, bf16[128,1024]{1,0:T(8,128)(2,1)}, u32[]{:S(2)}, u32[]{:S(2)}) collective-permute-start(bf16[128,1024]{1,0:T(8,128)(2,1)} %collective-permute-done.1), channel_id=1, source_target_pairs={{0,1},{1,2},{2,3},{3,4},{4,5},{5,6},{6,7},{7,8},{8,9},{9,10},{10,1... | collective-permute-start | bytes 786440 | tf_op jit(solution)/shard_map/ppermute | solution.py:16
  59.8 12.1 %collective-permute-start.6 = (bf16[128,1024]{1,0:T(8,128)(2,1)}, bf16[128,1024]{1,0:T(8,128)(2,1)}, u32[]{:S(2)}, u32[]{:S(2)}) collective-permute-start(bf16[128,1024]{1,0:T(8,128)(2,1)} %collective-permute-done.5), channel_id=1, source_target_pairs={{1,0},{2,1},{3,2},{4,3},{5,4},{6,5},{7,6},{8,7},{9,8},{10,9},{11,1... | collective-permute-start | bytes 786440 | tf_op jit(solution)/shard_map/ppermute | solution.py:16
  61.1 12.0 %collective-permute-start.3 = (bf16[128,1024]{1,0:T(8,128)(2,1)}, bf16[128,1024]{1,0:T(8,128)(2,1)}, u32[]{:S(2)}, u32[]{:S(2)}) collective-permute-start(bf16[128,1024]{1,0:T(8,128)(2,1)} %collective-permute-done.2), channel_id=1, source_target_pairs={{0,1},{1,2},{2,3},{3,4},{4,5},{5,6},{6,7},{7,8},{8,9},{9,10},{10,1... | collective-permute-start | bytes 786440 | tf_op jit(solution)/shard_map/ppermute | solution.py:16
  71.9 15.8 %collective-permute-start.7 = (bf16[128,1024]{1,0:T(8,128)(2,1)}, bf16[128,1024]{1,0:T(8,128)(2,1)S(1)}, u32[]{:S(2)}, u32[]{:S(2)}) collective-permute-start(bf16[128,1024]{1,0:T(8,128)(2,1)} %collective-permute-done.6), channel_id=1, source_target_pairs={{1,0},{2,1},{3,2},{4,3},{5,4},{6,5},{7,6},{8,7},{9,8},{10,9},{11,1... | collective-permute-start | bytes 786440 | tf_op jit(solution)/shard_map/ppermute | solution.py:16
  73.2 9.4 %slice-start = ((s8[6291456]{0:T(1024)(128)(4,1)}), s8[4194304]{0:T(1024)(128)(4,1)S(1)}, s32[]{:S(2)}) async-start(s8[6291456]{0:T(1024)(128)(4,1)} %bitcast.101), calls=%async_computation.5 | async-start | bytes 8388608
  76.3 6.2 %slice-start.1 = ((s8[6291456]{0:T(1024)(128)(4,1)}), s8[2097152]{0:T(1024)(128)(4,1)S(1)}, s32[]{:S(2)}) async-start(s8[6291456]{0:T(1024)(128)(4,1)} %bitcast.101), calls=%async_computation.6 | async-start | bytes 4194304
  76.3 6.2 %copy-start.10 = (bf16[128,1024]{1,0:T(8,128)(2,1)S(1)}, bf16[128,1024]{1,0:T(8,128)(2,1)}, u32[]{:S(2)}) copy-start(bf16[128,1024]{1,0:T(8,128)(2,1)} %copy-done.9) | copy-start | bytes 786436
  82.5 1.0 copy-start.8
  88.4 2.1 copy-start.3
  95.2 8.4 %copy-start.4 = (bf16[128,1024]{0,1:T(8,128)(2,1)S(1)}, bf16[128,1024]{0,1:T(8,128)(2,1)}, u32[]{:S(2)}) copy-start(bf16[128,1024]{0,1:T(8,128)(2,1)} %copy.27) | copy-start | bytes 786436
  109.1 4.2 %copy-start.2 = (bf16[128,1024]{1,0:T(8,128)(2,1)S(1)}, bf16[128,1024]{1,0:T(8,128)(2,1)}, u32[]{:S(2)}) copy-start(bf16[128,1024]{1,0:T(8,128)(2,1)} %param.15) | copy-start | bytes 786436
  126.0 4.6 %copy-start.5 = (bf16[128,1024]{0,1:T(8,128)(2,1)S(1)}, bf16[128,1024]{0,1:T(8,128)(2,1)}, u32[]{:S(2)}) copy-start(bf16[128,1024]{0,1:T(8,128)(2,1)} %copy.27) | copy-start | bytes 786436
  190.1 2.1 copy-start.1
  193.8 22.8 %collective-permute-start.8 = (bf16[128,2048]{1,0:T(8,128)(2,1)S(1)}, bf16[128,2048]{1,0:T(8,128)(2,1)}, u32[]{:S(2)}, u32[]{:S(2)}) collective-permute-start(bf16[128,2048]{1,0:T(8,128)(2,1)S(1)} %get-tuple-element.8), channel_id=1, source_target_pairs={{0,1},{1,2},{2,3},{3,4},{4,5},{5,6},{6,7},{7,8},{8,9},{9,10},{10,1... | collective-permute-start | bytes 1572872 | tf_op jit(solution)/shard_map/ppermute | solution.py:16
  199.3 19.2 %collective-permute-start.15 = (bf16[128,2048]{1,0:T(8,128)(2,1)S(1)}, bf16[128,2048]{1,0:T(8,128)(2,1)}, u32[]{:S(2)}, u32[]{:S(2)}) collective-permute-start(bf16[128,2048]{1,0:T(8,128)(2,1)S(1)} %get-tuple-element.9), channel_id=1, source_target_pairs={{4,0},{5,1},{6,2},{7,3},{8,4},{9,5},{10,6},{11,7},{12,8},{13,9},{1... | collective-permute-start | bytes 1572872 | tf_op jit(solution)/shard_map/ppermute | solution.py:16
  200.5 22.8 %collective-permute-start.14 = (bf16[128,2048]{1,0:T(8,128)(2,1)S(1)}, bf16[128,2048]{1,0:T(8,128)(2,1)}, u32[]{:S(2)}, u32[]{:S(2)}) collective-permute-start(bf16[128,2048]{1,0:T(8,128)(2,1)S(1)} %get-tuple-element.10), channel_id=1, source_target_pairs={{0,4},{1,5},{2,6},{3,7},{4,8},{5,9},{6,10},{7,11},{8,12},{9,13},{1... | collective-permute-start | bytes 1572872 | tf_op jit(solution)/shard_map/ppermute | solution.py:16
  208.3 35.6 %collective-permute-start.13 = (bf16[128,2048]{1,0:T(8,128)(2,1)}, bf16[128,2048]{1,0:T(8,128)(2,1)}, u32[]{:S(2)}, u32[]{:S(2)}) collective-permute-start(bf16[128,2048]{1,0:T(8,128)(2,1)} %get-tuple-element.11), channel_id=1, source_target_pairs={{3,0},{4,1},{5,2},{6,3},{7,4},{8,5},{9,6},{10,7},{11,8},{12,9},{13... | collective-permute-start | bytes 1572872 | tf_op jit(solution)/shard_map/ppermute | solution.py:16
  209.8 35.9 %collective-permute-start.12 = (bf16[128,2048]{1,0:T(8,128)(2,1)}, bf16[128,2048]{1,0:T(8,128)(2,1)}, u32[]{:S(2)}, u32[]{:S(2)}) collective-permute-start(bf16[128,2048]{1,0:T(8,128)(2,1)} %get-tuple-element.12), channel_id=1, source_target_pairs={{0,3},{1,4},{2,5},{3,6},{4,7},{5,8},{6,9},{7,10},{8,11},{9,12},{10... | collective-permute-start | bytes 1572872 | tf_op jit(solution)/shard_map/ppermute | solution.py:16
  216.6 29.2 %collective-permute-start.11 = (bf16[128,2048]{1,0:T(8,128)(2,1)}, bf16[128,2048]{1,0:T(8,128)(2,1)}, u32[]{:S(2)}, u32[]{:S(2)}) collective-permute-start(bf16[128,2048]{1,0:T(8,128)(2,1)} %get-tuple-element.13), channel_id=1, source_target_pairs={{2,0},{3,1},{4,2},{5,3},{6,4},{7,5},{8,6},{9,7},{10,8},{11,9},{12,... | collective-permute-start | bytes 1572872 | tf_op jit(solution)/shard_map/ppermute | solution.py:16
  218.4 36.5 %collective-permute-start.10 = (bf16[128,2048]{1,0:T(8,128)(2,1)}, bf16[128,2048]{1,0:T(8,128)(2,1)}, u32[]{:S(2)}, u32[]{:S(2)}) collective-permute-start(bf16[128,2048]{1,0:T(8,128)(2,1)} %get-tuple-element.14), channel_id=1, source_target_pairs={{0,2},{1,3},{2,4},{3,5},{4,6},{5,7},{6,8},{7,9},{8,10},{9,11},{10,... | collective-permute-start | bytes 1572872 | tf_op jit(solution)/shard_map/ppermute | solution.py:16
  223.3 31.6 %collective-permute-start.9 = (bf16[128,2048]{1,0:T(8,128)(2,1)}, bf16[128,2048]{1,0:T(8,128)(2,1)}, u32[]{:S(2)}, u32[]{:S(2)}) collective-permute-start(bf16[128,2048]{1,0:T(8,128)(2,1)} %get-tuple-element.15), channel_id=1, source_target_pairs={{1,0},{2,1},{3,2},{4,3},{5,4},{6,5},{7,6},{8,7},{9,8},{10,9},{11,1... | collective-permute-start | bytes 1572872 | tf_op jit(solution)/shard_map/ppermute | solution.py:16
  243.7 14.3 %copy-start.6 = (f32[1024]{0:T(1024)S(1)}, f32[1024]{0:T(1024)}, u32[]{:S(2)}) copy-start(f32[1024]{0:T(1024)} %param.12) | copy-start | bytes 12292
  265.0 40.7 %all-to-all-start.2 = ((bf16[16,8,1024]{2,1,0:T(8,128)(2,1)}), bf16[16,8,1024]{2,1,0:T(8,128)(2,1)S(1)}, u32[]{:S(2)}, u32[]{:S(2)}) async-start(bf16[16,8,1024]{2,1,0:T(8,128)(2,1)} %bitcast.33), calls=%async_computation.2 | async-start | bytes 524288 | tf_op jit(solution)/shard_map/all_to_all | solution.py:130
Sparse Core Ops, SparseCore 0:
  116.1 78.6 reduce-scatter.1
where the time goes:
time: 318 us; the launch traced here: 316 us
  matrix products  85.6 us (27%)
  blocking collectives  60.1 us (19%)
  starting transfers between devices  59.4 us (19%)
  local copies, waits for them, and re-layouts  50.4 us (16%)
  other arithmetic  33.8 us (11%)
  between operations  15.2 us (5%)
  waiting for transfers between devices  11.6 us (4%)
    ppermute x16, starting transfers between devices, from_behind(): return lax.ppermute(block, axis, route)  54.3 us
    psum x1, blocking collectives, per_device(): grad_gain = lax.psum(gain_term, 'ctx') * norm_scale  33.8 us
    dot_general x1, matrix products, per_device(): jnp.einsum('shqk,sqhd->skhd', d_scores, heads_q, preferred_element_type=j...  19.2 us
    dot_general x1, matrix products, per_device(): jnp.einsum('shqk,skhd->sqhd', d_scores, heads_k, preferred_element_type=j...  19.1 us
    dot_general x8, matrix products, per_device(): jnp.dot(remote_piece, kv_weight, preferred_element_type=jnp.float32)  14.8 us
    all_to_all x1, blocking collectives, per_device(): lax.all_to_all(wanted, 'ctx', split_axis=0, concat_axis=0, tiled=True)  13.6 us
    all_to_all x1, blocking collectives, per_device(): lax.all_to_all(outgoing, 'ctx', split_axis=0, concat_axis=0, tiled=True)  12.6 us
    scatter-add x1, other arithmetic, per_device(): jnp.zeros(window_blocks.shape, jnp.float32).at[slot_index.reshape(-1)]  11.9 us
  transfers between devices with their start and end apart: 18, of which 3 were waited for; matrix products, arithmetic and copies ran while one was open for 40% of the time, Pallas kernels for 0%

commit v1 on v0

--- a/solution.py
+++ b/solution.py
@@ -8,6 +8,12 @@
 REACH = 4
 EPS = 1e-06
 FAR = -1e30
+
+
+def add_all(block, name):
+    parts = lax.all_gather(block, name, axis=0, tiled=False)
+    result = parts.sum(axis=0)
+    return result
 
 
 def from_behind(block, axis, distance):
@@ -118,7 +124,7 @@
     d_proj = jnp.concatenate([d_query, d_kv], axis=-1)
     d_normed = jnp.dot(d_proj, w_qkv.T, preferred_element_type=jnp.float32)
     gain_term = jnp.sum(d_normed * ordered_f * inv_rms, axis=0)
-    grad_gain = lax.psum(gain_term, "ctx") * norm_scale
+    grad_gain = add_all(gain_term, "ctx") * norm_scale
     scaled = d_normed * norm_gain
     d_ordered = (
         cotangent.astype(jnp.float32)

time: 318 us -> 306 us (0.962)
  blocking collectives: 60.1 us -> 48.1 us
    psum x1 -> x0, blocking collectives: 33.8 us -> none  [per_device(): grad_gain = lax.psum(gain_term, 'ctx') * norm_scale]
    all_gather x0 -> x1, blocking collectives: none -> 21.9 us  [add_all(): parts = lax.all_gather(block, name, axis=0, tiled=False)]
  transfers between devices with their start and end apart: 18 -> 18, of which waited for: 3 -> 3; matrix products, arithmetic and copies ran while one was open for 40% -> 42% of each run, Pallas kernels for 0% -> 0%
where the time goes in v1:
time: 306 us; the launch traced here: 304 us
  matrix products  85.6 us (28%)
  starting transfers between devices  59.4 us (19%)
  local copies, waits for them, and re-layouts  50.4 us (16%)
  blocking collectives  48.1 us (16%)
  other arithmetic  33.8 us (11%)
  between operations  15.2 us (5%)
  waiting for transfers between devices  11.6 us (4%)
    ppermute x16, starting transfers between devices, from_behind(): return lax.ppermute(block, axis, route)  54.3 us
    all_gather x1, blocking collectives, add_all(): parts = lax.all_gather(block, name, axis=0, tiled=False)  21.9 us
    dot_general x1, matrix products, per_device(): jnp.einsum('shqk,sqhd->skhd', d_scores, heads_q, preferred_element_type=j...  19.2 us
    dot_general x1, matrix products, per_device(): jnp.einsum('shqk,skhd->sqhd', d_scores, heads_k, preferred_element_type=j...  19.1 us
    dot_general x8, matrix products, per_device(): jnp.dot(remote_piece, kv_weight, preferred_element_type=jnp.float32)  14.8 us
    all_to_all x1, blocking collectives, per_device(): lax.all_to_all(wanted, 'ctx', split_axis=0, concat_axis=0, tiled=True)  13.6 us
    all_to_all x1, blocking collectives, per_device(): lax.all_to_all(outgoing, 'ctx', split_axis=0, concat_axis=0, tiled=True)  12.6 us
    scatter-add x1, other arithmetic, per_device(): jnp.zeros(window_blocks.shape, jnp.float32).at[slot_index.reshape(-1)]  11.9 us
  transfers between devices with their start and end apart: 18, of which 3 were waited for; matrix products, arithmetic and copies ran while one was open for 42% of the time, Pallas kernels for 0%

profile of v1, /device:TPU:0, one launch (start us, length us, event | category | flops | bytes accessed | tf_op | source)
XLA Modules:
  0.0 304.1 jit_solution(10321079200044107415)
XLA Ops:
  7.2 0.8 and_select_fusion
  8.0 2.5 sort.17
  10.6 1.2 gather_fusion
  11.9 13.6 %all_to_all.19 = s32[16,1,8]{2,1,0:T(1,128)S(1)} all-to-all(s32[16,1,8]{2,1,0:T(1,128)S(1)} %bitcast.117), channel_id=1, replica_groups=mesh['groups'=2,'ctx'=16] {'ctx'}, dimensions={0} | all-to-all | bytes 1024 | tf_op jit(solution)/shard_map/all_to_all | solution.py:54
  26.9 2.0 gather_fusion.1
  28.9 12.6 %all_to_all.20 = bf16[16,8,1024]{2,1,0:T(8,128)(2,1)S(1)} all-to-all(bf16[16,8,1024]{2,1,0:T(8,128)(2,1)S(1)} %bitcast.109), channel_id=1, replica_groups=mesh['groups'=2,'ctx'=16] {'ctx'}, dimensions={0} | all-to-all | bytes 524288 | tf_op jit(solution)/shard_map/all_to_all | solution.py:57
  41.5 1.2 scatter_custom_fusion
  42.9 0.8 fusion.60
  43.7 1.8 collective-permute-start
  45.5 1.3 collective-permute-start.4
  46.8 4.6 %collective-permute-start.1 = (bf16[128,1024]{1,0:T(8,128)(2,1)S(1)}, bf16[128,1024]{1,0:T(8,128)(2,1)}, u32[]{:S(2)}, u32[]{:S(2)}) collective-permute-start(bf16[128,1024]{1,0:T(8,128)(2,1)S(1)} %collective-permute-done), channel_id=1, source_target_pairs={{0,1},{1,2},{2,3},{3,4},{4,5},{5,6},{6,7},{7,8},{8,9},{9,10},{10,1... | collective-permute-start | bytes 786440 | tf_op jit(solution)/shard_map/ppermute | solution.py:22
  51.4 1.3 collective-permute-start.5
  52.7 6.4 %collective-permute-start.2 = (bf16[128,1024]{1,0:T(8,128)(2,1)}, bf16[128,1024]{1,0:T(8,128)(2,1)}, u32[]{:S(2)}, u32[]{:S(2)}) collective-permute-start(bf16[128,1024]{1,0:T(8,128)(2,1)} %collective-permute-done.1), channel_id=1, source_target_pairs={{0,1},{1,2},{2,3},{3,4},{4,5},{5,6},{6,7},{7,8},{8,9},{9,10},{10,1... | collective-permute-start | bytes 786440 | tf_op jit(solution)/shard_map/ppermute | solution.py:22
  59.8 1.3 collective-permute-start.6
  61.1 6.1 %collective-permute-start.3 = (bf16[128,1024]{1,0:T(8,128)(2,1)}, bf16[128,1024]{1,0:T(8,128)(2,1)}, u32[]{:S(2)}, u32[]{:S(2)}) collective-permute-start(bf16[128,1024]{1,0:T(8,128)(2,1)} %collective-permute-done.2), channel_id=1, source_target_pairs={{0,1},{1,2},{2,3},{3,4},{4,5},{5,6},{6,7},{7,8},{8,9},{9,10},{10,1... | collective-permute-start | bytes 786440 | tf_op jit(solution)/shard_map/ppermute | solution.py:22
  67.2 3.8 %convolution_convert_fusion = bf16[128,3072]{1,0:T(8,128)(2,1)S(1)} fusion(bf16[128,1024]{1,0:T(8,128)(2,1)S(1)} %fusion.60, bf16[1024,3072]{1,0:T(8,128)(2,1)} %param.13), kind=kOutput, calls=%fused_computation.16 | convolution fusion | flops 805699584 | bytes 7340032 | tf_op jit(solution)/shard_map/dot_general | solution.py:64
  71.0 0.8 copy.34
  71.9 1.3 collective-permute-start.7
  73.2 3.1 %fusion.24 = bf16[1152,2048]{1,0:T(8,128)(2,1)S(1)} fusion(bf16[128,1024]{1,0:T(8,128)(2,1)} %collective-permute-done.3, bf16[1024,3072]{1,0:T(8,128)(2,1)} %param.13), kind=kOutput, calls=%fused_computation.40 | convolution fusion | flops 537133056 | bytes 4980736 | tf_op jit(solution)/shard_map/dot_general | solution.py:78
  76.3 3.1 %fusion.23 = bf16[1152,2048]{1,0:T(8,128)(2,1)S(1)} fusion(bf16[1152,2048]{1,0:T(8,128)(2,1)S(1)} %fusion.24, bf16[128,1024]{1,0:T(8,128)(2,1)} %collective-permute-done.2, bf16[1024,3072]{1,0:T(8,128)(2,1)} %param.13), kind=kOutput, calls=%fused_computation.38 | convolution fusion | flops 537133056 | bytes 4980736 | tf_op jit(solution)/shard_map/dot_general | solution.py:78
  79.5 3.0 fusion.22
  82.6 0.7 fusion.21
  84.2 1.7 fusion.19
  85.9 1.7 fusion.18
  88.4 2.1 copy-done.3
  90.5 4.7 %gather_fusion.2 = bf16[5,128,2048]{2,1,0:T(8,128)(2,1)} fusion(bf16[9,128,2048]{2,1,0:T(8,128)(2,1)} %bitcast.106, s32[1024]{0:T(1024)S(1)} %pad_clamp_fusion), kind=kCustom, calls=%fused_computation.2 | custom fusion | bytes 5242900 | tf_op jit(solution)/shard_map/gather | solution.py:88
  95.2 3.5 %fusion.89 = (bf16[1,640,1024]{2,1,0:T(8,128)(2,1)}, bf16[1,640,1024]{2,1,0:T(8,128)(2,1)}) fusion(bf16[1,640,2048]{2,1,0:T(8,128)(2,1)} %bitcast.103), kind=kLoop, calls=%fused_computation.138 | loop fusion | bytes 5242880 | tf_op jit(solution)/shard_map/slice | solution.py:89
  98.7 2.5 copy.40
  101.1 2.5 copy.39
  103.6 5.5 %fusion.90 = (f32[16,128]{1,0:T(8,128)S(1)}, f32[16,128,640]{2,1,0:T(8,128)}) fusion(pred[640]{0:T(1024)(128)(4,1)S(1)} %fusion.75, bf16[128,16,64]{0,2,1:T(8,128)(2,1)S(1)} %bitcast.114, bf16[640,16,64]{0,2,1:T(8,128)(2,1)} %bitcast.107), kind=kOutput, calls=%fused_computation.139 | convolution fusion | flops 173015680 | bytes 6824576 | tf_op jit(solution)/shard_map/sub | solution.py:34
  109.2 4.1 %fusion.31 = bf16[16,64,128]{2,1,0:T(8,128)(2,1)S(1)} fusion(bf16[640,16,64]{0,2,1:T(8,128)(2,1)} %bitcast.104, f32[16,128,640]{2,1,0:T(8,128)} %get-tuple-element.23, f32[16,128]{1,0:T(8,128)S(1)} %get-tuple-element.22), kind=kOutput, calls=%fused_computation.47 | convolution fusion | flops 170524672 | bytes 6823936 | tf_op jit(solution)/shard_map/shqk,skhd->sqhd/dot_general | solution.py:94
  113.3 2.7 fusion.92
  116.0 0.8 convolution_convert_fusion.9
  117.0 4.6 %convolution_bitcast_fusion = f32[1,640,16,64]{1,3,2,0:T(8,128)} fusion(bf16[128,16,64]{0,2,1:T(8,128)(2,1)S(1)} %bitcast.112, f32[16,128,640]{2,1,0:T(8,128)} %get-tuple-element.23, f32[16,128]{1,0:T(8,128)S(1)} %get-tuple-element.22), kind=kOutput, calls=%fused_computation.42 | convolution fusion | flops 170393600 | bytes 8134656 | tf_op jit(solution)/shard_map/shqk,sqhd->skhd/dot_general | solution.py:109
  121.6 4.4 %reshape.226 = f32[5,128,1024]{1,0,2:T(8,128)} reshape(f32[1,640,16,64]{1,3,2,0:T(8,128)} %convolution_bitcast_fusion) | data formatting | bytes 5242880 | tf_op jit(solution)/shard_map/reshape | solution.py:111
  126.0 4.6 %fusion.91 = f32[16,128,640]{2,1,0:T(8,128)} fusion(bf16[128,16,64]{0,2,1:T(8,128)(2,1)S(1)} %bitcast.113, bf16[640,16,64]{0,2,1:T(8,128)(2,1)} %bitcast.105), kind=kOutput, calls=%fused_computation.140 | convolution fusion | flops 167772160 | bytes 6815744 | tf_op jit(solution)/shard_map/sqhd,skhd->shqk/dot_general | solution.py:103
  130.6 19.2 %fusion.25 = f32[1,640,16,64]{1,3,2,0:T(8,128)} fusion(bf16[128,16,64]{0,2,1:T(8,128)(2,1)S(1)} %bitcast.115, f32[16,128,640]{2,1,0:T(8,128)} %fusion.91, f32[16,128,640]{2,1,0:T(8,128)} %get-tuple-element.23, f32[16,128]{1,0:T(8,128)S(1)} %get-tuple-element.22), kind=kOutput, calls=%fused_computation.41 | convolution fusion | flops 176949888 | bytes 13377536 | tf_op jit(solution)/shard_map/shqk,sqhd->skhd/dot_general | solution.py:108
  149.9 4.4 %reshape.225 = f32[5,128,1024]{1,0,2:T(8,128)} reshape(f32[1,640,16,64]{1,3,2,0:T(8,128)} %fusion.25) | data formatting | bytes 5242880 | tf_op jit(solution)/shard_map/reshape | solution.py:111
  154.3 6.7 %pad_maximum_fusion = f32[5,128,2048]{1,0,2:T(8,128)} fusion(f32[5,128,1024]{1,0,2:T(8,128)} %reshape.226, f32[5,128,1024]{1,0,2:T(8,128)} %reshape.225), kind=kLoop, calls=%fused_computation.9 | loop fusion | flops 1310720 | bytes 10485760 | tf_op jit(solution)/shard_map/concatenate | solution.py:110
  161.0 7.9 %copy.37 = f32[5,128,2048]{2,1,0:T(8,128)} copy(f32[5,128,2048]{1,0,2:T(8,128)} %pad_maximum_fusion) | data formatting | bytes 10485760 | tf_op jit(solution)/shard_map/concatenate | solution.py:110
  168.9 4.8 %broadcast_in_dim.22 = f32[9,128,2048]{2,1,0:T(8,128)} broadcast(f32[]{:T(128)} %constant.63.clone.1), dimensions={} | broadcast | bytes 9437188 | tf_op jit(solution)/shard_map/broadcast_in_dim | solution.py:113
  173.7 11.9 %scatter_fusion = f32[9,128,2048]{2,1,0:T(8,128)} fusion(f32[9,128,2048]{2,1,0:T(8,128)} %broadcast_in_dim.22, s32[5]{0:T(128)S(1)} %fusion.81, f32[5,128,2048]{2,1,0:T(8,128)} %copy.37), kind=kCustom, calls=%fused_computation.5 | custom fusion | flops 1310720 | bytes 15728660 | tf_op jit(solution)/shard_map/scatter-add | solution.py:113
  185.7 4.4 %convert_element_type.137 = bf16[9,128,2048]{2,1,0:T(8,128)(2,1)S(1)} convert(f32[9,128,2048]{2,1,0:T(8,128)} %scatter_fusion) | non-fusion elementwise | flops 2359296 | bytes 14155776 | tf_op jit(solution)/shard_map/convert_element_type | solution.py:114
  190.1 2.1 copy-done.1
  192.2 1.6 slice_bitcast_fusion.7
  193.8 5.4 %collective-permute-start.8 = (bf16[128,2048]{1,0:T(8,128)(2,1)S(1)}, bf16[128,2048]{1,0:T(8,128)(2,1)}, u32[]{:S(2)}, u32[]{:S(2)}) collective-permute-start(bf16[128,2048]{1,0:T(8,128)(2,1)S(1)} %get-tuple-element.8), channel_id=1, source_target_pairs={{0,1},{1,2},{2,3},{3,4},{4,5},{5,6},{6,7},{7,8},{8,9},{9,10},{10,1... | collective-permute-start | bytes 1572872 | tf_op jit(solution)/shard_map/ppermute | solution.py:22
  199.3 1.3 collective-permute-start.15
  200.5 7.8 %collective-permute-start.14 = (bf16[128,2048]{1,0:T(8,128)(2,1)S(1)}, bf16[128,2048]{1,0:T(8,128)(2,1)}, u32[]{:S(2)}, u32[]{:S(2)}) collective-permute-start(bf16[128,2048]{1,0:T(8,128)(2,1)S(1)} %get-tuple-element.10), channel_id=1, source_target_pairs={{0,4},{1,5},{2,6},{3,7},{4,8},{5,9},{6,10},{7,11},{8,12},{9,13},{1... | collective-permute-start | bytes 1572872 | tf_op jit(solution)/shard_map/ppermute | solution.py:22
  208.3 1.5 collective-permute-start.13
  209.8 6.8 %collective-permute-start.12 = (bf16[128,2048]{1,0:T(8,128)(2,1)}, bf16[128,2048]{1,0:T(8,128)(2,1)}, u32[]{:S(2)}, u32[]{:S(2)}) collective-permute-start(bf16[128,2048]{1,0:T(8,128)(2,1)} %get-tuple-element.12), channel_id=1, source_target_pairs={{0,3},{1,4},{2,5},{3,6},{4,7},{5,8},{6,9},{7,10},{8,11},{9,12},{10... | collective-permute-start | bytes 1572872 | tf_op jit(solution)/shard_map/ppermute | solution.py:22
  216.6 1.3 collective-permute-start.11
  218.4 4.9 %collective-permute-start.10 = (bf16[128,2048]{1,0:T(8,128)(2,1)}, bf16[128,2048]{1,0:T(8,128)(2,1)}, u32[]{:S(2)}, u32[]{:S(2)}) collective-permute-start(bf16[128,2048]{1,0:T(8,128)(2,1)} %get-tuple-element.14), channel_id=1, source_target_pairs={{0,2},{1,3},{2,4},{3,5},{4,6},{5,7},{6,8},{7,9},{8,10},{9,11},{10,... | collective-permute-start | bytes 1572872 | tf_op jit(solution)/shard_map/ppermute | solution.py:22
  223.3 1.3 collective-permute-start.9
  224.6 19.1 %fusion.34 = bf16[16,64,128]{2,1,0:T(8,128)(2,1)S(1)} fusion(bf16[640,16,64]{0,2,1:T(8,128)(2,1)} %bitcast.108, f32[16,128,640]{2,1,0:T(8,128)} %fusion.91, f32[16,128,640]{2,1,0:T(8,128)} %get-tuple-element.23, f32[16,128]{1,0:T(8,128)S(1)} %get-tuple-element.22), kind=kOutput, calls=%fused_computation.48 | convolution fusion | flops 177080960 | bytes 12066816 | tf_op jit(solution)/shard_map/shqk,skhd->sqhd/dot_general | solution.py:106
  243.9 1.9 collective-permute-done.12
  245.8 9.2 %collective-permute-done.10 = bf16[128,2048]{1,0:T(8,128)(2,1)} collective-permute-done((bf16[128,2048]{1,0:T(8,128)(2,1)}, bf16[128,2048]{1,0:T(8,128)(2,1)}, u32[]{:S(2)}, u32[]{:S(2)}) %collective-permute-start.10) | collective-permute-done | bytes 524320 | tf_op jit(solution)/shard_map/ppermute | solution.py:22
  255.0 3.1 %fusion.45 = bf16[128,2048]{1,0:T(8,128)(2,1)S(1)} fusion(bf16[128,2048]{1,0:T(8,128)(2,1)} %collective-permute-done.15, bf16[128,2048]{1,0:T(8,128)(2,1)} %collective-permute-done.14, bf16[128,2048]{1,0:T(8,128)(2,1)} %collective-permute-done.13, bf16[128,2048]{1,0:T(8,128)(2,1)} %collective-permute-done.12, bf16[128,2048]{1,0:T(8,128)(2,1)} %collective-permute-done.11, ...), kind=kLoop, calls=%fused_computation.64 | loop fusion | flops 4718592 | bytes 5242880 | tf_op jit(solution)/shard_map/convert_element_type | solution.py:123
  258.0 5.1 %fusion.66 = (f32[1024]{0:T(1024)S(1)}, f32[128]{0:T(128)S(1)}, f32[128,1024]{1,0:T(8,128)S(1)}) fusion(bf16[128,1024]{1,0:T(8,128)(2,1)S(1)} %scatter_custom_fusion, f32[128]{0:T(128)S(1)} %get-tuple-element.19, f32[1024]{0:T(1024)S(1)} %copy-done.6, bf16[1024,3072]{1,0:T(8,128)(2,1)} %param.13, bf16[128,2048]{1,0:T(8,128)(2,1)S(1)} %fusion.45, ...), kind=kOutput, calls=%fused_computation.85 | convolution fusion | flops 807795584 | bytes 7873536 | tf_op jit(solution)/shard_map/dot_general | solution.py:125
  263.4 1.6 gather_fusion.3
  265.0 5.1 %all-to-all-start.2 = ((bf16[16,8,1024]{2,1,0:T(8,128)(2,1)}), bf16[16,8,1024]{2,1,0:T(8,128)(2,1)S(1)}, u32[]{:S(2)}, u32[]{:S(2)}) async-start(bf16[16,8,1024]{2,1,0:T(8,128)(2,1)} %bitcast.33), calls=%async_computation.2 | async-start | bytes 524288 | tf_op jit(solution)/shard_map/all_to_all | solution.py:136
  270.1 1.2 fusion.37
  271.3 21.9 %all-gather = f32[16384]{0:T(1024)S(1)} all-gather(f32[1024]{0:T(1024)S(1)} %get-tuple-element.6), channel_id=2, replica_groups=mesh['groups'=2,'ctx'=16] {'ctx'}, dimensions={0}, use_global_device_ids=true | all-gather | bytes 69632 | tf_op jit(solution)/shard_map/all_gather | solution.py:14
  293.8 1.8 scatter_custom_fusion.2
  295.6 1.7 broadcast_multiply_fusion
  (71 shorter events, 5.1 us)
Async XLA Ops:
  7.2 108.8 %copy-start = (bf16[1024,1024]{1,0:T(8,128)(2,1)S(1)}, bf16[1024,1024]{1,0:T(8,128)(2,1)}, u32[]{:S(2)}) copy-start(bf16[1024,1024]{1,0:T(8,128)(2,1)} %param.14) | copy-start | bytes 6291460
  7.2 51.9 %copy-start.11 = (s32[1,5]{1,0:T(1,128)S(1)}, s32[1,5]{1,0:T(1,128)}, u32[]{:S(2)}) copy-start(s32[1,5]{1,0:T(1,128)} %param.10) | copy-start | bytes 64
  7.2 288.4 %reduce-scatter.2.cloned.1.call-start = ((), (), s32[]{:S(2)}) async-start(), calls=%async_computation.4 | async-start | bytes 4456448 | tf_op jit(solution)/shard_map/reduce_scatter | solution.py:143
  43.7 3.1 %collective-permute-start = (bf16[128,1024]{1,0:T(8,128)(2,1)S(1)}, bf16[128,1024]{1,0:T(8,128)(2,1)S(1)}, u32[]{:S(2)}, u32[]{:S(2)}) collective-permute-start(bf16[128,1024]{1,0:T(8,128)(2,1)S(1)} %fusion.60), channel_id=1, source_target_pairs={{0,1},{1,2},{2,3},{3,4},{4,5},{5,6},{6,7},{7,8},{8,9},{9,10},{10,1... | collective-permute-start | bytes 786440 | tf_op jit(solution)/shard_map/ppermute | solution.py:22
  45.5 5.9 %collective-permute-start.4 = (bf16[128,1024]{1,0:T(8,128)(2,1)S(1)}, bf16[128,1024]{1,0:T(8,128)(2,1)S(1)}, u32[]{:S(2)}, u32[]{:S(2)}) collective-permute-start(bf16[128,1024]{1,0:T(8,128)(2,1)S(1)} %fusion.60), channel_id=1, source_target_pairs={{1,0},{2,1},{3,2},{4,3},{5,4},{6,5},{7,6},{8,7},{9,8},{10,9},{11,1... | collective-permute-start | bytes 786440 | tf_op jit(solution)/shard_map/ppermute | solution.py:22
  46.8 14.3 %copy-start.9 = (bf16[128,1024]{1,0:T(8,128)(2,1)}, bf16[128,1024]{1,0:T(8,128)(2,1)S(1)}, u32[]{:S(2)}) copy-start(bf16[128,1024]{1,0:T(8,128)(2,1)S(1)} %collective-permute-done) | copy-start | bytes 786436
  46.8 5.9 %collective-permute-start.1 = (bf16[128,1024]{1,0:T(8,128)(2,1)S(1)}, bf16[128,1024]{1,0:T(8,128)(2,1)}, u32[]{:S(2)}, u32[]{:S(2)}) collective-permute-start(bf16[128,1024]{1,0:T(8,128)(2,1)S(1)} %collective-permute-done), channel_id=1, source_target_pairs={{0,1},{1,2},{2,3},{3,4},{4,5},{5,6},{6,7},{7,8},{8,9},{9,10},{10,1... | collective-permute-start | bytes 786440 | tf_op jit(solution)/shard_map/ppermute | solution.py:22
  51.4 9.7 %copy-start.7 = (bf16[128,1024]{1,0:T(8,128)(2,1)}, bf16[128,1024]{1,0:T(8,128)(2,1)S(1)}, u32[]{:S(2)}) copy-start(bf16[128,1024]{1,0:T(8,128)(2,1)S(1)} %collective-permute-done.4) | copy-start | bytes 786436
  51.4 8.4 %collective-permute-start.5 = (bf16[128,1024]{1,0:T(8,128)(2,1)S(1)}, bf16[128,1024]{1,0:T(8,128)(2,1)}, u32[]{:S(2)}, u32[]{:S(2)}) collective-permute-start(bf16[128,1024]{1,0:T(8,128)(2,1)S(1)} %collective-permute-done.4), channel_id=1, source_target_pairs={{1,0},{2,1},{3,2},{4,3},{5,4},{6,5},{7,6},{8,7},{9,8},{10,9},{11,1... | collective-permute-start | bytes 786440 | tf_op jit(solution)/shard_map/ppermute | solution.py:22
  52.7 8.4 %collective-permute-start.2 = (bf16[128,1024]{1,0:T(8,128)(2,1)}, bf16[128,1024]{1,0:T(8,128)(2,1)}, u32[]{:S(2)}, u32[]{:S(2)}) collective-permute-start(bf16[128,1024]{1,0:T(8,128)(2,1)} %collective-permute-done.1), channel_id=1, source_target_pairs={{0,1},{1,2},{2,3},{3,4},{4,5},{5,6},{6,7},{7,8},{8,9},{9,10},{10,1... | collective-permute-start | bytes 786440 | tf_op jit(solution)/shard_map/ppermute | solution.py:22
  59.8 12.1 %collective-permute-start.6 = (bf16[128,1024]{1,0:T(8,128)(2,1)}, bf16[128,1024]{1,0:T(8,128)(2,1)}, u32[]{:S(2)}, u32[]{:S(2)}) collective-permute-start(bf16[128,1024]{1,0:T(8,128)(2,1)} %collective-permute-done.5), channel_id=1, source_target_pairs={{1,0},{2,1},{3,2},{4,3},{5,4},{6,5},{7,6},{8,7},{9,8},{10,9},{11,1... | collective-permute-start | bytes 786440 | tf_op jit(solution)/shard_map/ppermute | solution.py:22
  61.1 12.0 %collective-permute-start.3 = (bf16[128,1024]{1,0:T(8,128)(2,1)}, bf16[128,1024]{1,0:T(8,128)(2,1)}, u32[]{:S(2)}, u32[]{:S(2)}) collective-permute-start(bf16[128,1024]{1,0:T(8,128)(2,1)} %collective-permute-done.2), channel_id=1, source_target_pairs={{0,1},{1,2},{2,3},{3,4},{4,5},{5,6},{6,7},{7,8},{8,9},{9,10},{10,1... | collective-permute-start | bytes 786440 | tf_op jit(solution)/shard_map/ppermute | solution.py:22
  71.9 15.8 %collective-permute-start.7 = (bf16[128,1024]{1,0:T(8,128)(2,1)}, bf16[128,1024]{1,0:T(8,128)(2,1)S(1)}, u32[]{:S(2)}, u32[]{:S(2)}) collective-permute-start(bf16[128,1024]{1,0:T(8,128)(2,1)} %collective-permute-done.6), channel_id=1, source_target_pairs={{1,0},{2,1},{3,2},{4,3},{5,4},{6,5},{7,6},{8,7},{9,8},{10,9},{11,1... | collective-permute-start | bytes 786440 | tf_op jit(solution)/shard_map/ppermute | solution.py:22
  73.2 9.4 %slice-start = ((s8[6291456]{0:T(1024)(128)(4,1)}), s8[4194304]{0:T(1024)(128)(4,1)S(1)}, s32[]{:S(2)}) async-start(s8[6291456]{0:T(1024)(128)(4,1)} %bitcast.101), calls=%async_computation.5 | async-start | bytes 8388608
  76.3 6.2 %slice-start.1 = ((s8[6291456]{0:T(1024)(128)(4,1)}), s8[2097152]{0:T(1024)(128)(4,1)S(1)}, s32[]{:S(2)}) async-start(s8[6291456]{0:T(1024)(128)(4,1)} %bitcast.101), calls=%async_computation.6 | async-start | bytes 4194304
  76.3 6.2 %copy-start.10 = (bf16[128,1024]{1,0:T(8,128)(2,1)S(1)}, bf16[128,1024]{1,0:T(8,128)(2,1)}, u32[]{:S(2)}) copy-start(bf16[128,1024]{1,0:T(8,128)(2,1)} %copy-done.9) | copy-start | bytes 786436
  82.5 1.0 copy-start.8
  88.4 2.1 copy-start.3
  95.2 8.4 %copy-start.4 = (bf16[128,1024]{0,1:T(8,128)(2,1)S(1)}, bf16[128,1024]{0,1:T(8,128)(2,1)}, u32[]{:S(2)}) copy-start(bf16[128,1024]{0,1:T(8,128)(2,1)} %copy.34) | copy-start | bytes 786436
  109.1 4.2 %copy-start.2 = (bf16[128,1024]{1,0:T(8,128)(2,1)S(1)}, bf16[128,1024]{1,0:T(8,128)(2,1)}, u32[]{:S(2)}) copy-start(bf16[128,1024]{1,0:T(8,128)(2,1)} %param.15) | copy-start | bytes 786436
  126.0 4.6 %copy-start.5 = (bf16[128,1024]{0,1:T(8,128)(2,1)S(1)}, bf16[128,1024]{0,1:T(8,128)(2,1)}, u32[]{:S(2)}) copy-start(bf16[128,1024]{0,1:T(8,128)(2,1)} %copy.34) | copy-start | bytes 786436
  190.1 2.1 copy-start.1
  193.8 22.8 %collective-permute-start.8 = (bf16[128,2048]{1,0:T(8,128)(2,1)S(1)}, bf16[128,2048]{1,0:T(8,128)(2,1)}, u32[]{:S(2)}, u32[]{:S(2)}) collective-permute-start(bf16[128,2048]{1,0:T(8,128)(2,1)S(1)} %get-tuple-element.8), channel_id=1, source_target_pairs={{0,1},{1,2},{2,3},{3,4},{4,5},{5,6},{6,7},{7,8},{8,9},{9,10},{10,1... | collective-permute-start | bytes 1572872 | tf_op jit(solution)/shard_map/ppermute | solution.py:22
  199.3 19.2 %collective-permute-start.15 = (bf16[128,2048]{1,0:T(8,128)(2,1)S(1)}, bf16[128,2048]{1,0:T(8,128)(2,1)}, u32[]{:S(2)}, u32[]{:S(2)}) collective-permute-start(bf16[128,2048]{1,0:T(8,128)(2,1)S(1)} %get-tuple-element.9), channel_id=1, source_target_pairs={{4,0},{5,1},{6,2},{7,3},{8,4},{9,5},{10,6},{11,7},{12,8},{13,9},{1... | collective-permute-start | bytes 1572872 | tf_op jit(solution)/shard_map/ppermute | solution.py:22
  200.5 22.8 %collective-permute-start.14 = (bf16[128,2048]{1,0:T(8,128)(2,1)S(1)}, bf16[128,2048]{1,0:T(8,128)(2,1)}, u32[]{:S(2)}, u32[]{:S(2)}) collective-permute-start(bf16[128,2048]{1,0:T(8,128)(2,1)S(1)} %get-tuple-element.10), channel_id=1, source_target_pairs={{0,4},{1,5},{2,6},{3,7},{4,8},{5,9},{6,10},{7,11},{8,12},{9,13},{1... | collective-permute-start | bytes 1572872 | tf_op jit(solution)/shard_map/ppermute | solution.py:22
  208.3 35.6 %collective-permute-start.13 = (bf16[128,2048]{1,0:T(8,128)(2,1)}, bf16[128,2048]{1,0:T(8,128)(2,1)}, u32[]{:S(2)}, u32[]{:S(2)}) collective-permute-start(bf16[128,2048]{1,0:T(8,128)(2,1)} %get-tuple-element.11), channel_id=1, source_target_pairs={{3,0},{4,1},{5,2},{6,3},{7,4},{8,5},{9,6},{10,7},{11,8},{12,9},{13... | collective-permute-start | bytes 1572872 | tf_op jit(solution)/shard_map/ppermute | solution.py:22
  209.8 35.9 %collective-permute-start.12 = (bf16[128,2048]{1,0:T(8,128)(2,1)}, bf16[128,2048]{1,0:T(8,128)(2,1)}, u32[]{:S(2)}, u32[]{:S(2)}) collective-permute-start(bf16[128,2048]{1,0:T(8,128)(2,1)} %get-tuple-element.12), channel_id=1, source_target_pairs={{0,3},{1,4},{2,5},{3,6},{4,7},{5,8},{6,9},{7,10},{8,11},{9,12},{10... | collective-permute-start | bytes 1572872 | tf_op jit(solution)/shard_map/ppermute | solution.py:22
  216.6 29.2 %collective-permute-start.11 = (bf16[128,2048]{1,0:T(8,128)(2,1)}, bf16[128,2048]{1,0:T(8,128)(2,1)}, u32[]{:S(2)}, u32[]{:S(2)}) collective-permute-start(bf16[128,2048]{1,0:T(8,128)(2,1)} %get-tuple-element.13), channel_id=1, source_target_pairs={{2,0},{3,1},{4,2},{5,3},{6,4},{7,5},{8,6},{9,7},{10,8},{11,9},{12,... | collective-permute-start | bytes 1572872 | tf_op jit(solution)/shard_map/ppermute | solution.py:22
  218.4 36.5 %collective-permute-start.10 = (bf16[128,2048]{1,0:T(8,128)(2,1)}, bf16[128,2048]{1,0:T(8,128)(2,1)}, u32[]{:S(2)}, u32[]{:S(2)}) collective-permute-start(bf16[128,2048]{1,0:T(8,128)(2,1)} %get-tuple-element.14), channel_id=1, source_target_pairs={{0,2},{1,3},{2,4},{3,5},{4,6},{5,7},{6,8},{7,9},{8,10},{9,11},{10,... | collective-permute-start | bytes 1572872 | tf_op jit(solution)/shard_map/ppermute | solution.py:22
  223.3 31.6 %collective-permute-start.9 = (bf16[128,2048]{1,0:T(8,128)(2,1)}, bf16[128,2048]{1,0:T(8,128)(2,1)}, u32[]{:S(2)}, u32[]{:S(2)}) collective-permute-start(bf16[128,2048]{1,0:T(8,128)(2,1)} %get-tuple-element.15), channel_id=1, source_target_pairs={{1,0},{2,1},{3,2},{4,3},{5,4},{6,5},{7,6},{8,7},{9,8},{10,9},{11,1... | collective-permute-start | bytes 1572872 | tf_op jit(solution)/shard_map/ppermute | solution.py:22
  243.7 14.3 %copy-start.6 = (f32[1024]{0:T(1024)S(1)}, f32[1024]{0:T(1024)}, u32[]{:S(2)}) copy-start(f32[1024]{0:T(1024)} %param.12) | copy-start | bytes 12292
  265.0 28.8 %all-to-all-start.2 = ((bf16[16,8,1024]{2,1,0:T(8,128)(2,1)}), bf16[16,8,1024]{2,1,0:T(8,128)(2,1)S(1)}, u32[]{:S(2)}, u32[]{:S(2)}) async-start(bf16[16,8,1024]{2,1,0:T(8,128)(2,1)} %bitcast.33), calls=%async_computation.2 | async-start | bytes 524288 | tf_op jit(solution)/shard_map/all_to_all | solution.py:136
Sparse Core Ops, SparseCore 0:
  116.1 78.6 reduce-scatter.1
